TPU v7x, 128 devices: a whole 4x4x4 slice. The times are simulated.
128 devices in a mesh: req: 32 (over x, z, core), mlp: 4 (over y).
Axes of the slice: x: 4, y: 4, z: 4, core: 2. Of those that a mesh axis runs over, the one named last changes fastest.
Arguments:
- queries: bfloat16 [16896, 2048], P('req', 'mlp'), may hold values from -6 to 6
- key_cache: bfloat16 [2560, 128, 1024], P('req', None, 'mlp'), may hold values from -6 to 6
- value_cache: bfloat16 [2560, 128, 1024], P('req', None, 'mlp'), may hold values from -6 to 6
- decode_len: int32 [512], P('req'), may hold values from 1 to 4096, as said below
- stretch_start: int32 [32], P('req'), may hold values from 0 to 3584, as said below
- page_table: int32 [544, 32], P('req'), may hold values from 0 to 79, as said below
- hidden_in: bfloat16 [16896, 2304], P('req')
- o_weight: bfloat16 [2048, 2304], P('mlp'), may hold values from -0.125 to 0.125
- attn_gain: float32 [2304], replicated, may hold values from 0.1 to 1.9
- ffn_in_gain: float32 [2304], replicated, may hold values from 0.1 to 1.9
- ffn_out_gain: float32 [2304], replicated, may hold values from 0.1 to 1.9
- w_gate: bfloat16 [2304, 9216], P('req', 'mlp'), may hold values from -0.125 to 0.125
- w_up: bfloat16 [2304, 9216], P('req', 'mlp'), may hold values from -0.125 to 0.125
- w_down: bfloat16 [2304, 9216], P('req', 'mlp')
Outputs:
- layer_out: bfloat16 [16896, 2304], P('req', 'mlp')
Inputs may be any that keep to these rules, and one draw needn't show every extreme that they name: `decode_len`: each decode request's tokens fill its first pages; request 1 of req index 1 holds 4096 tokens. `stretch_start`: req index 0 starts at 3584, req index 1 at 0. `page_table`: row j of req index r's block of 17 rows names request j's pages by slot in that index's own pool of 80 pages; the slots holding a req index's tokens are all distinct; entries past a request's last page are valid slots that hold none of its tokens.
All inputs are finite; a program needn't handle non-finite values.
Results may differ from a plain program's by a relative error of at most 0.014.
Values may be sent and summed in bfloat16 or wider, within the bound.
A program may use at most 128 MiB of HBM per device.

v0:
```python
import math
import jax
import jax.numpy as jnp
from jax import lax
from jax.sharding import PartitionSpec as P

H = 8
KVH = 4
HD = 256
PRE_DEV = 512
DEC_DEV = 16
EPS = 1e-06
CAP = 50.0


def rms(values, gain):
    return values * lax.rsqrt(jnp.mean(values * values, axis=-1, keepdims=True) + EPS) * gain


def capped_weight(scores, visible):
    capped = CAP * jnp.tanh(scores / (16.0 * CAP))
    return jnp.where(visible, jnp.exp(capped), jnp.float32(0.0))


def attend(queries, key_cache, value_cache, decode_len, stretch_start, page_table):
    rows = queries.shape[0]
    local_kv = key_cache.shape[2] // HD
    rep = H // KVH
    pool = key_cache.shape[0]
    page_len = key_cache.shape[1]
    max_pages = page_table.shape[1]
    query = queries.reshape(rows, local_kv, rep, HD)
    pre_q = query[:PRE_DEV]
    dec_q = query[PRE_DEV:]
    start = stretch_start[0]
    pre_keys = key_cache[page_table[0]].reshape(max_pages * page_len, local_kv, HD)
    pre_vals = value_cache[page_table[0]].reshape(max_pages * page_len, local_kv, HD)
    position = jnp.arange(max_pages * page_len, dtype=jnp.int32)
    limit = start + jnp.arange(PRE_DEV, dtype=jnp.int32) + 1
    pre_scores = jnp.einsum("rghd,tgd->rght", pre_q, pre_keys, preferred_element_type=jnp.float32)
    pre_weight = capped_weight(
        pre_scores, position[None, None, None, :] < limit[:, None, None, None]
    )
    pre_num = jnp.einsum(
        "rght,tgd->rghd",
        pre_weight.astype(jnp.bfloat16),
        pre_vals,
        preferred_element_type=jnp.float32,
    )
    pre_den = jnp.sum(pre_weight, axis=-1)
    table = page_table[1:]
    page_idx = jnp.arange(max_pages, dtype=jnp.int32)
    used = page_idx[None, :] * page_len < decode_len[:, None]
    owned = (table[:, :, None] == jnp.arange(pool, dtype=jnp.int32)[None, None, :]) & used[
        :, :, None
    ]
    base = jnp.min(jnp.where(owned, page_idx[None, :, None] * page_len, jnp.int32(1 << 30)), axis=1)
    dec_pos = (base[:, :, None] + jnp.arange(page_len, dtype=jnp.int32)[None, None, :]).reshape(
        DEC_DEV, pool * page_len
    )
    all_keys = key_cache.reshape(pool * page_len, local_kv, HD)
    all_vals = value_cache.reshape(pool * page_len, local_kv, HD)
    dec_scores = jnp.einsum("rghd,tgd->rght", dec_q, all_keys, preferred_element_type=jnp.float32)
    dec_weight = capped_weight(dec_scores, (dec_pos < decode_len[:, None])[:, None, None, :])
    dec_num = jnp.einsum(
        "rght,tgd->rghd",
        dec_weight.astype(jnp.bfloat16),
        all_vals,
        preferred_element_type=jnp.float32,
    )
    dec_den = jnp.sum(dec_weight, axis=-1)
    pre_out = (pre_num / pre_den[..., None]).astype(jnp.bfloat16)
    dec_out = (dec_num / dec_den[..., None]).astype(jnp.bfloat16)
    return jnp.concatenate([pre_out, dec_out], axis=0).reshape(rows, local_kv * rep * HD)


def per_device(
    queries,
    key_cache,
    value_cache,
    decode_len,
    stretch_start,
    page_table,
    hidden_in,
    o_weight,
    attn_gain,
    ffn_in_gain,
    ffn_out_gain,
    w_gate,
    w_up,
    w_down,
):
    attended = attend(queries, key_cache, value_cache, decode_len, stretch_start, page_table)
    projected = lax.psum(
        jnp.dot(attended, o_weight, preferred_element_type=jnp.float32).astype(jnp.bfloat16), "mlp"
    ).astype(jnp.float32)
    resid = hidden_in.astype(jnp.float32) + rms(projected, attn_gain)
    normed = rms(resid, ffn_in_gain).astype(jnp.bfloat16)
    gate = jnp.dot(
        normed,
        lax.all_gather(w_gate, "req", axis=0, tiled=True),
        preferred_element_type=jnp.float32,
    )
    up_part = jnp.dot(
        normed, lax.all_gather(w_up, "req", axis=0, tiled=True), preferred_element_type=jnp.float32
    )
    act = (jax.nn.gelu(gate, approximate=True) * up_part).astype(jnp.bfloat16)
    partial_out = lax.dot_general(
        act,
        lax.all_gather(w_down, "req", axis=0, tiled=True),
        (((1,), (1,)), ((), ())),
        preferred_element_type=jnp.float32,
    )
    width = hidden_in.shape[1] // lax.axis_size("mlp")
    first = lax.axis_index("mlp") * width
    total = lax.psum(partial_out.astype(jnp.bfloat16), "mlp").astype(jnp.float32)
    combined = resid + rms(total, ffn_out_gain)
    result = lax.dynamic_slice_in_dim(combined, first, width, 1)
    return result.astype(jnp.bfloat16)


def solution(mesh):
    return jax.shard_map(
        per_device,
        mesh=mesh,
        in_specs=(
            P("req", "mlp"),
            P("req", None, "mlp"),
            P("req", None, "mlp"),
            P("req"),
            P("req"),
            P("req", None),
            P("req", None),
            P("mlp", None),
            P(),
            P(),
            P(),
            P("req", "mlp"),
            P("req", "mlp"),
            P("req", "mlp"),
        ),
        out_specs=P("req", "mlp"),
        check_vma=False,
    )
```

profile of v0, /device:TPU:1, one launch (start us, length us, event | category | flops | bytes accessed | tf_op | source)
XLA Modules:
  0.0 324.8 jit_solution(14163465529039394121)
XLA Ops:
  7.4 0.8 fusion.41
  8.2 0.7 slice.17
  8.9 1.1 slice.16
  10.7 3.0 iota_compare_fusion
  13.7 0.2 copy.35
  13.9 4.5 %gather_fusion.1 = bf16[32,128,256]{2,1,0:T(8,128)(2,1)} fusion(bf16[80,128,256]{2,1,0:T(8,128)(2,1)} %param.15, s32[1024]{0:T(1024)S(1)} %pad_clamp_fusion), kind=kCustom, calls=%fused_computation.1 | custom fusion | bytes 4194432 | tf_op jit(solution)/shard_map/gather | solution.py:36
  18.4 4.5 %gather_fusion = bf16[32,128,256]{2,1,0:T(8,128)(2,1)} fusion(bf16[80,128,256]{2,1,0:T(8,128)(2,1)} %param.16, s32[1024]{0:T(1024)S(1)} %pad_clamp_fusion), kind=kCustom, calls=%fused_computation | custom fusion | bytes 4194432 | tf_op jit(solution)/shard_map/gather | solution.py:37
  22.9 0.1 broadcast_compare_fusion
  23.0 0.2 select_reduce_fusion
  23.2 0.2 add.106
  23.5 0.3 fusion.35
  23.8 0.0 slice-start
  23.8 0.0 slice-start.2
  23.8 10.4 %fusion = (f32[512,2]{0,1:T(2,128)S(1)}, f32[4096,512,2]{1,0,2:T(8,128)}) fusion(pred[512,4096]{0,1:T(8,128)(4,1)} %iota_compare_fusion, bf16[4096,256,1]{1,0,2:T(8,128)(2,1)} %bitcast.101, bf16[512,2,256]{0,2,1:T(8,128)(2,1)S(1)} %bitcast.110), kind=kOutput, calls=%fused_computation.3 | convolution fusion | flops 2164259840 | bytes 21499904 | tf_op jit(solution)/shard_map/rghd,tgd->rght/dot_general | solution.py:40
  34.2 0.0 copy-done.3
  34.2 0.0 slice-start.1
  34.2 0.0 slice-start.4
  34.3 0.0 slice-start.3
  34.3 9.5 %fusion.32 = bf16[512,1,2,256]{0,3,2,1:T(8,128)(2,1)S(1)} fusion(bf16[4096,256,1]{1,0,2:T(8,128)(2,1)S(1)} %bitcast.100, f32[4096,512,2]{1,0,2:T(8,128)} %get-tuple-element.10, pred[512,4096]{0,1:T(8,128)(4,1)S(1)} %copy-done.2, f32[512,2]{0,1:T(2,128)S(1)} %get-tuple-element.9), kind=kOutput, calls=%fused_computation.45 | convolution fusion | flops 2164785152 | bytes 21499904 | tf_op jit(solution)/shard_map/rght,tgd->rghd/dot_general | solution.py:44
  43.9 1.8 fusion.47
  45.6 2.1 fusion.29
  47.8 0.1 pad_maximum_fusion
  47.9 2.9 convolution_convert_fusion.1
  50.7 0.0 all-reduce.3.cloned.1.call-update
  50.8 0.0 all-gather.4.cloned.1.call-start
  50.8 0.5 all-gather.4.cloned.1.call-update
  51.4 0.0 all-gather.6.cloned.1.call-start
  51.4 0.5 all-gather.6.cloned.1.call-update
  51.9 0.0 all-gather.8.cloned.1.call-start
  52.0 0.5 all-gather.8.cloned.1.call-update
  52.5 0.0 all-reduce.5.cloned.1.call-start
  52.6 65.7 %all-reduce.3.cloned.1.call-done = bf16[528,2304]{1,0:T(8,128)(2,1)} async-done(((bf16[528,2304]{1,0:T(8,128)(2,1)}), bf16[528,2304]{1,0:T(8,128)(2,1)}) %all-reduce.3.cloned.1.call-update) | async-done | bytes 2433040 | tf_op jit(solution)/shard_map/psum | solution.py:94
  118.2 2.2 fusion.11
  120.5 0.0 copy-start.6
  120.5 5.8 %multiply_reduce_fusion.1 = (f32[528]{0:T(1024)S(1)}, f32[528,2304]{1,0:T(8,128)}) fusion(f32[2304]{0:T(1024)S(1)} %copy-done.4, f32[528]{0:T(1024)S(1)} %add_rsqrt_fusion.2, bf16[528,2304]{1,0:T(8,128)(2,1)} %all-reduce.3.cloned.1.call-done, bf16[528,2304]{1,0:T(8,128)(2,1)} %param.20), kind=kLoop, calls=%fused_computation.31 | loop fusion | flops 8515056 | bytes 9745536 | tf_op jit(solution)/shard_map/reduce_sum | solution.py:17
  126.3 0.0 copy-done.6
  126.3 12.7 %fusion.45 = f32[528,2304]{1,0:T(8,128)} fusion(bf16[2304,2304]{1,0:T(8,128)(2,1)} %all-gather.4.cloned.1.call-done, f32[528,2304]{1,0:T(8,128)} %get-tuple-element.6, f32[2304]{0:T(1024)S(1)} %copy-done.6, f32[528]{0:T(1024)S(1)} %add_rsqrt_fusion.1), kind=kOutput, calls=%fused_computation.69 | convolution fusion | flops 5609336832 | bytes 20360256 | tf_op jit(solution)/shard_map/dot_general | solution.py:99
  139.0 36.0 %all-gather.6.cloned.1.call-done = bf16[2304,2304]{1,0:T(8,128)(2,1)} async-done(((bf16[72,2304]{1,0:T(8,128)(2,1)}), bf16[2304,2304]{1,0:T(8,128)(2,1)}) %all-gather.6.cloned.1.call-update) | async-done | bytes 10616848 | tf_op jit(solution)/shard_map/all_gather | solution.py:105
  175.0 12.9 %fusion.21 = bf16[528,2304]{1,0:T(8,128)(2,1)} fusion(bf16[2304,2304]{1,0:T(8,128)(2,1)} %all-gather.6.cloned.1.call-done, f32[528,2304]{1,0:T(8,128)} %fusion.45, f32[528,2304]{1,0:T(8,128)} %get-tuple-element.6, f32[2304]{0:T(1024)S(1)} %copy-done.6, f32[528]{0:T(1024)S(1)} %add_rsqrt_fusion.1), kind=kOutput, calls=%fused_computation.32 | convolution fusion | flops 5621501952 | bytes 22793280 | tf_op jit(solution)/shard_map/dot_general | solution.py:104
  187.8 46.8 %all-gather.8.cloned.1.call-done = bf16[2304,2304]{1,0:T(8,128)(2,1)} async-done(((bf16[72,2304]{1,0:T(8,128)(2,1)}), bf16[2304,2304]{1,0:T(8,128)(2,1)}) %all-gather.8.cloned.1.call-update) | async-done | bytes 10616848 | tf_op jit(solution)/shard_map/all_gather | solution.py:110
  234.7 11.6 %convolution_convert_fusion = bf16[528,2304]{1,0:T(8,128)(2,1)} fusion(bf16[528,2304]{1,0:T(8,128)(2,1)} %fusion.21, bf16[2304,2304]{1,0:T(8,128)(2,1)} %all-gather.8.cloned.1.call-done), kind=kOutput, calls=%fused_computation.33 | convolution fusion | flops 5606903808 | bytes 15482880 | tf_op jit(solution)/shard_map/dot_general | solution.py:108
  246.3 0.0 all-reduce.5.cloned.1.call-update
  246.3 0.8 dynamic-slice
  247.1 62.5 %all-reduce.5.cloned.1.call-done = bf16[528,2304]{1,0:T(8,128)(2,1)} async-done(((bf16[528,2304]{1,0:T(8,128)(2,1)}), bf16[528,2304]{1,0:T(8,128)(2,1)}) %all-reduce.5.cloned.1.call-update) | async-done | bytes 2433040 | tf_op jit(solution)/shard_map/psum | solution.py:116
  309.6 2.2 multiply_reduce_fusion
  311.8 0.0 copy-start.1
  311.9 2.2 convert_element_type.54
  314.1 3.2 fusion.25
  (26 shorter events, 0.1 us)
Async XLA Ops:
  7.4 40.5 %copy-start = (bf16[512,2304]{1,0:T(8,128)(2,1)S(1)}, bf16[512,2304]{1,0:T(8,128)(2,1)}, u32[]{:S(2)}) copy-start(bf16[512,2304]{1,0:T(8,128)(2,1)} %param.21) | copy-start | bytes 7077892
  7.4 110.9 %all-reduce.3.cloned.1.call-start = ((), (), s32[]{:S(2)}) async-start(), calls=%async_computation | async-start | bytes 4866048 | tf_op jit(solution)/shard_map/psum | solution.py:94
  13.7 9.2 %copy-start.5 = (s32[16]{0:T(128)S(1)}, s32[16]{0:T(128)}, u32[]{:S(2)}) copy-start(s32[16]{0:T(128)} %param.17) | copy-start | bytes 196
  23.7 10.5 %copy-start.2 = (pred[512,4096]{0,1:T(8,128)(4,1)S(1)}, pred[512,4096]{0,1:T(8,128)(4,1)}, u32[]{:S(2)}) copy-start(pred[512,4096]{0,1:T(8,128)(4,1)} %iota_compare_fusion) | copy-start | bytes 6291460
  23.7 10.5 %copy-start.3 = (bf16[32,128,256]{2,1,0:T(8,128)(2,1)S(1)}, bf16[32,128,256]{2,1,0:T(8,128)(2,1)}, u32[]{:S(2)}) copy-start(bf16[32,128,256]{2,1,0:T(8,128)(2,1)} %gather_fusion) | copy-start | bytes 6291460
  23.8 20.1 %slice-start = ((s8[5242880]{0:T(1024)(128)(4,1)}), s8[4194304]{0:T(1024)(128)(4,1)S(1)}, s32[]{:S(2)}) async-start(s8[5242880]{0:T(1024)(128)(4,1)} %bitcast.102), calls=%async_computation.5 | async-start | bytes 8388608
  23.8 21.8 %slice-start.2 = ((s8[5242880]{0:T(1024)(128)(4,1)}), s8[4194304]{0:T(1024)(128)(4,1)S(1)}, s32[]{:S(2)}) async-start(s8[5242880]{0:T(1024)(128)(4,1)} %bitcast.105), calls=%async_computation.7 | async-start | bytes 8388608
  34.2 9.6 %slice-start.1 = ((s8[5242880]{0:T(1024)(128)(4,1)}), s8[1048576]{0:T(1024)(128)(4,1)S(1)}, s32[]{:S(2)}) async-start(s8[5242880]{0:T(1024)(128)(4,1)} %bitcast.102), calls=%async_computation.6 | async-start | bytes 2097152
  34.2 9.6 %slice-start.4 = ((bf16[528,512]{1,0:T(8,128)(2,1)}), bf16[16,512]{1,0:T(8,128)(2,1)S(1)}, s32[]{:S(2)}) async-start(bf16[528,512]{1,0:T(8,128)(2,1)} %param.14), calls=%async_computation.9 | async-start | bytes 32768 | tf_op jit(solution)/shard_map/slice | solution.py:34
  34.3 11.4 %slice-start.3 = ((s8[5242880]{0:T(1024)(128)(4,1)}), s8[1048576]{0:T(1024)(128)(4,1)S(1)}, s32[]{:S(2)}) async-start(s8[5242880]{0:T(1024)(128)(4,1)} %bitcast.105), calls=%async_computation.8 | async-start | bytes 2097152
  50.7 69.7 %copy-start.4 = (f32[2304]{0:T(1024)S(1)}, f32[2304]{0:T(1024)}, u32[]{:S(2)}) copy-start(f32[2304]{0:T(1024)} %param.22) | copy-start | bytes 27652
  50.8 75.5 %all-gather.4.cloned.1.call-start = ((), (), s32[]{:S(2)}) async-start(), calls=%async_computation.1 | async-start | bytes 10948608 | tf_op jit(solution)/shard_map/all_gather | solution.py:101
  51.4 123.6 %all-gather.6.cloned.1.call-start = ((), (), s32[]{:S(2)}) async-start(), calls=%async_computation.2 | async-start | bytes 10948608 | tf_op jit(solution)/shard_map/all_gather | solution.py:105
  51.9 182.7 %all-gather.8.cloned.1.call-start = ((), (), s32[]{:S(2)}) async-start(), calls=%async_computation.3 | async-start | bytes 10948608 | tf_op jit(solution)/shard_map/all_gather | solution.py:110
  52.5 257.1 %all-reduce.5.cloned.1.call-start = ((), (), s32[]{:S(2)}) async-start(), calls=%async_computation.4 | async-start | bytes 4866048 | tf_op jit(solution)/shard_map/psum | solution.py:116
  120.5 5.8 %copy-start.6 = (f32[2304]{0:T(1024)S(1)}, f32[2304]{0:T(1024)}, u32[]{:S(2)}) copy-start(f32[2304]{0:T(1024)} %param.23) | copy-start | bytes 27652
  311.8 5.4 %copy-start.1 = (bf16[512,2304]{1,0:T(8,128)(2,1)S(1)}, bf16[512,2304]{1,0:T(8,128)(2,1)}, u32[]{:S(2)}) copy-start(bf16[512,2304]{1,0:T(8,128)(2,1)} %param.21) | copy-start | bytes 7077892
Sparse Core Ops, SparseCore 0:
  50.9 67.3 all-reduce.2
  246.4 63.1 all-reduce.4
Sparse Core Ops, SparseCore 1:
  53.6 61.6 all-gather.3
  117.4 57.5 all-gather.5
  177.2 57.4 all-gather.7
where the time goes:
time: 325 us
  waiting for transfers between devices  213 us (66%)
  matrix products  63.9 us (20%)
  other arithmetic  20.2 us (6%)
  between operations  15.9 us (5%)
  local copies, waits for them, and re-layouts  12 us (4%)
    psum x1, waiting for transfers between devices, per_device(): lax.psum(jnp.dot(attended, o_weight, preferred_element_type=jnp.float32)....  65.7 us
    psum x1, waiting for transfers between devices, per_device(): lax.psum(partial_out.astype(jnp.bfloat16), 'mlp').astype(jnp.float32)  62.5 us
    all_gather x1, waiting for transfers between devices, per_device(): lax.all_gather(w_down, 'req', axis=0, tiled=True)  46.8 us
    all_gather x1, waiting for transfers between devices, per_device(): lax.all_gather(w_up, 'req', axis=0, tiled=True)  36 us
    dot_general x1, matrix products, per_device(): jnp.dot(normed, lax.all_gather(w_up, 'req', axis=0, tiled=True), preferre...  12.9 us
    dot_general x1, matrix products, per_device(): jnp.dot(normed, lax.all_gather(w_gate, 'req', axis=0, tiled=True), prefer...  12.7 us
    dot_general x1, matrix products, per_device(): lax.dot_general(act, lax.all_gather(w_down, 'req', axis=0, tiled=True), (...  11.6 us
    dot_general x1, matrix products, attend(): jnp.einsum('rghd,tgd->rght', pre_q, pre_keys, preferred_element_type=jnp....  10.4 us
  transfers between devices with their start and end apart: 5, of which 4 were waited for; matrix products, arithmetic and copies ran while one was open for 11% of the time, Pallas kernels for 0%

commit v1 on v0

--- a/solution.py
+++ b/solution.py
@@ -113,7 +113,9 @@
     )
     width = hidden_in.shape[1] // lax.axis_size("mlp")
     first = lax.axis_index("mlp") * width
-    total = lax.psum(partial_out.astype(jnp.bfloat16), "mlp").astype(jnp.float32)
+    total = jnp.sum(lax.all_gather(partial_out.astype(jnp.bfloat16), "mlp"), axis=0).astype(
+        jnp.float32
+    )
     combined = resid + rms(total, ffn_out_gain)
     result = lax.dynamic_slice_in_dim(combined, first, width, 1)
     return result.astype(jnp.bfloat16)

time: 325 us -> 361 us (1.11)
  waiting for transfers between devices: 213 us -> 243 us
  other arithmetic: 20.2 us -> 26 us
    all_gather x0 -> x1, waiting for transfers between devices: none -> 92.7 us  [per_device(): lax.all_gather(partial_out.astype(jnp.bfloat16), 'mlp')]
    psum x1 -> x0, waiting for transfers between devices: 62.5 us -> none  [per_device(): lax.psum(partial_out.astype(jnp.bfloat16), 'mlp').astype(jnp.float32)]
    reduce_sum x0 -> x1, other arithmetic: none -> 7.56 us  [per_device(): jnp.sum(lax.all_gather(partial_out.astype(jnp.bfloat16), 'mlp'), axis=0)]
  transfers between devices with their start and end apart: 5 -> 5, of which waited for: 4 -> 4; matrix products, arithmetic and copies ran while one was open for 11% -> 10% of each run, Pallas kernels for 0% -> 0%
where the time goes in v1:
time: 361 us
  waiting for transfers between devices  243 us (67%)
  matrix products  63.9 us (18%)
  other arithmetic  26 us (7%)
  between operations  15.9 us (4%)
  local copies, waits for them, and re-layouts  12.3 us (3%)
    all_gather x1, waiting for transfers between devices, per_device(): lax.all_gather(partial_out.astype(jnp.bfloat16), 'mlp')  92.7 us
    psum x1, waiting for transfers between devices, per_device(): lax.psum(jnp.dot(attended, o_weight, preferred_element_type=jnp.float32)....  65.7 us
    all_gather x1, waiting for transfers between devices, per_device(): lax.all_gather(w_down, 'req', axis=0, tiled=True)  46.8 us
    all_gather x1, waiting for transfers between devices, per_device(): lax.all_gather(w_up, 'req', axis=0, tiled=True)  36 us
    dot_general x1, matrix products, per_device(): jnp.dot(normed, lax.all_gather(w_up, 'req', axis=0, tiled=True), preferre...  12.9 us
    dot_general x1, matrix products, per_device(): jnp.dot(normed, lax.all_gather(w_gate, 'req', axis=0, tiled=True), prefer...  12.7 us
    dot_general x1, matrix products, per_device(): lax.dot_general(act, lax.all_gather(w_down, 'req', axis=0, tiled=True), (...  11.6 us
    dot_general x1, matrix products, attend(): jnp.einsum('rghd,tgd->rght', pre_q, pre_keys, preferred_element_type=jnp....  10.4 us
  transfers between devices with their start and end apart: 5, of which 4 were waited for; matrix products, arithmetic and copies ran while one was open for 10% of the time, Pallas kernels for 0%

profile of v1, /device:TPU:1, one launch (start us, length us, event | category | flops | bytes accessed | tf_op | source)
XLA Modules:
  0.0 361.0 jit_solution(14327271495713828298)
XLA Ops:
  7.4 0.8 fusion.41
  8.2 0.7 slice.17
  8.9 1.1 slice.16
  10.7 3.0 iota_compare_fusion
  13.7 0.2 copy.35
  13.9 4.5 %gather_fusion.1 = bf16[32,128,256]{2,1,0:T(8,128)(2,1)} fusion(bf16[80,128,256]{2,1,0:T(8,128)(2,1)} %param.15, s32[1024]{0:T(1024)S(1)} %pad_clamp_fusion), kind=kCustom, calls=%fused_computation.1 | custom fusion | bytes 4194432 | tf_op jit(solution)/shard_map/gather | solution.py:36
  18.4 4.5 %gather_fusion = bf16[32,128,256]{2,1,0:T(8,128)(2,1)} fusion(bf16[80,128,256]{2,1,0:T(8,128)(2,1)} %param.16, s32[1024]{0:T(1024)S(1)} %pad_clamp_fusion), kind=kCustom, calls=%fused_computation | custom fusion | bytes 4194432 | tf_op jit(solution)/shard_map/gather | solution.py:37
  22.9 0.1 broadcast_compare_fusion
  23.0 0.2 select_reduce_fusion
  23.2 0.2 add.104
  23.5 0.3 fusion.35
  23.7 0.0 slice-start
  23.8 0.0 slice-start.2
  23.8 10.4 %fusion = (f32[512,2]{0,1:T(2,128)S(1)}, f32[4096,512,2]{1,0,2:T(8,128)}) fusion(pred[512,4096]{0,1:T(8,128)(4,1)} %iota_compare_fusion, bf16[4096,256,1]{1,0,2:T(8,128)(2,1)} %bitcast.103, bf16[512,2,256]{0,2,1:T(8,128)(2,1)S(1)} %bitcast.112), kind=kOutput, calls=%fused_computation.3 | convolution fusion | flops 2164259840 | bytes 21499904 | tf_op jit(solution)/shard_map/rghd,tgd->rght/dot_general | solution.py:40
  34.2 0.0 slice-start.1
  34.2 0.0 slice-start.4
  34.2 0.0 slice-start.3
  34.3 9.5 %fusion.32 = bf16[512,1,2,256]{0,3,2,1:T(8,128)(2,1)S(1)} fusion(bf16[4096,256,1]{1,0,2:T(8,128)(2,1)S(1)} %bitcast.102, f32[4096,512,2]{1,0,2:T(8,128)} %get-tuple-element.10, pred[512,4096]{0,1:T(8,128)(4,1)S(1)} %copy-done.3, f32[512,2]{0,1:T(2,128)S(1)} %get-tuple-element.9), kind=kOutput, calls=%fused_computation.45 | convolution fusion | flops 2164785152 | bytes 21499904 | tf_op jit(solution)/shard_map/rght,tgd->rghd/dot_general | solution.py:44
  43.9 1.8 fusion.47
  45.6 2.1 fusion.29
  47.8 0.1 pad_maximum_fusion
  47.9 2.9 convolution_convert_fusion.1
  50.7 0.0 all-reduce.2.cloned.1.call-update
  50.8 0.0 all-gather.6.cloned.1.call-start
  50.8 0.5 all-gather.6.cloned.1.call-update
  51.3 0.0 all-gather.8.cloned.1.call-start
  51.4 0.5 all-gather.8.cloned.1.call-update
  51.9 0.0 all-gather.10.cloned.1.call-start
  52.0 0.5 all-gather.10.cloned.1.call-update
  52.5 0.0 all-gather.12.cloned.1.call-start
  52.6 65.7 %all-reduce.2.cloned.1.call-done = bf16[528,2304]{1,0:T(8,128)(2,1)} async-done(((bf16[528,2304]{1,0:T(8,128)(2,1)}), bf16[528,2304]{1,0:T(8,128)(2,1)}) %all-reduce.2.cloned.1.call-update) | async-done | bytes 2433040 | tf_op jit(solution)/shard_map/psum | solution.py:94
  118.2 2.2 fusion.11
  120.5 0.0 copy-start.7
  120.5 5.8 %multiply_reduce_fusion.1 = (f32[528]{0:T(1024)S(1)}, f32[528,2304]{1,0:T(8,128)}) fusion(f32[2304]{0:T(1024)S(1)} %copy-done.5, f32[528]{0:T(1024)S(1)} %add_rsqrt_fusion.2, bf16[528,2304]{1,0:T(8,128)(2,1)} %all-reduce.2.cloned.1.call-done, bf16[528,2304]{1,0:T(8,128)(2,1)} %param.20), kind=kLoop, calls=%fused_computation.31 | loop fusion | flops 8515056 | bytes 9745536 | tf_op jit(solution)/shard_map/reduce_sum | solution.py:17
  126.3 12.7 %fusion.45 = f32[528,2304]{1,0:T(8,128)} fusion(bf16[2304,2304]{1,0:T(8,128)(2,1)} %all-gather.6.cloned.1.call-done, f32[528,2304]{1,0:T(8,128)} %get-tuple-element.6, f32[2304]{0:T(1024)S(1)} %copy-done.7, f32[528]{0:T(1024)S(1)} %add_rsqrt_fusion.1), kind=kOutput, calls=%fused_computation.69 | convolution fusion | flops 5609336832 | bytes 20360256 | tf_op jit(solution)/shard_map/dot_general | solution.py:99
  139.0 36.0 %all-gather.8.cloned.1.call-done = bf16[2304,2304]{1,0:T(8,128)(2,1)} async-done(((bf16[72,2304]{1,0:T(8,128)(2,1)}), bf16[2304,2304]{1,0:T(8,128)(2,1)}) %all-gather.8.cloned.1.call-update) | async-done | bytes 10616848 | tf_op jit(solution)/shard_map/all_gather | solution.py:105
  174.9 12.9 %fusion.21 = bf16[528,2304]{1,0:T(8,128)(2,1)} fusion(bf16[2304,2304]{1,0:T(8,128)(2,1)} %all-gather.8.cloned.1.call-done, f32[528,2304]{1,0:T(8,128)} %fusion.45, f32[528,2304]{1,0:T(8,128)} %get-tuple-element.6, f32[2304]{0:T(1024)S(1)} %copy-done.7, f32[528]{0:T(1024)S(1)} %add_rsqrt_fusion.1), kind=kOutput, calls=%fused_computation.32 | convolution fusion | flops 5621501952 | bytes 22793280 | tf_op jit(solution)/shard_map/dot_general | solution.py:104
  187.8 46.8 %all-gather.10.cloned.1.call-done = bf16[2304,2304]{1,0:T(8,128)(2,1)} async-done(((bf16[72,2304]{1,0:T(8,128)(2,1)}), bf16[2304,2304]{1,0:T(8,128)(2,1)}) %all-gather.10.cloned.1.call-update) | async-done | bytes 10616848 | tf_op jit(solution)/shard_map/all_gather | solution.py:110
  234.6 11.6 %convolution_convert_fusion = bf16[528,2304]{1,0:T(8,128)(2,1)} fusion(bf16[528,2304]{1,0:T(8,128)(2,1)} %fusion.21, bf16[2304,2304]{1,0:T(8,128)(2,1)} %all-gather.10.cloned.1.call-done), kind=kOutput, calls=%fused_computation.33 | convolution fusion | flops 5606903808 | bytes 15482880 | tf_op jit(solution)/shard_map/dot_general | solution.py:108
  246.2 0.0 all-gather.12.cloned.1.call-update
  246.2 0.8 dynamic-slice
  247.0 92.7 %all-gather.12.cloned.1.call-done = bf16[2112,2304]{1,0:T(8,128)(2,1)} async-done(((bf16[528,2304]{1,0:T(8,128)(2,1)}), bf16[2112,2304]{1,0:T(8,128)(2,1)}) %all-gather.12.cloned.1.call-update) | async-done | bytes 9732112 | tf_op jit(solution)/shard_map/all_gather | solution.py:116
  339.7 7.6 %reduce_sum.61 = bf16[528,2304]{1,0:T(8,128)(2,1)} reduce(bf16[4,528,2304]{2,1,0:T(8,128)(2,1)} %bitcast.100, bf16[]{:T(256)} %constant.18.clone.1), dimensions={0}, to_apply=%region_6.7 | reduce | flops 3649536 | bytes 12165122 | tf_op jit(solution)/shard_map/reduce_sum | solution.py:116
  347.3 2.2 convert_element_type.56
  349.5 0.2 copy-done.2
  349.7 0.5 multiply_reduce_fusion
  350.2 3.2 fusion.25
  353.4 0.0 copy-done.1
  (29 shorter events, 0.1 us)
Async XLA Ops:
  7.4 40.5 %copy-start = (bf16[512,2304]{1,0:T(8,128)(2,1)S(1)}, bf16[512,2304]{1,0:T(8,128)(2,1)}, u32[]{:S(2)}) copy-start(bf16[512,2304]{1,0:T(8,128)(2,1)} %param.21) | copy-start | bytes 7077892
  7.4 110.8 %all-reduce.2.cloned.1.call-start = ((), (), s32[]{:S(2)}) async-start(), calls=%async_computation | async-start | bytes 4866048 | tf_op jit(solution)/shard_map/psum | solution.py:94
  13.7 9.2 %copy-start.6 = (s32[16]{0:T(128)S(1)}, s32[16]{0:T(128)}, u32[]{:S(2)}) copy-start(s32[16]{0:T(128)} %param.17) | copy-start | bytes 196
  23.7 10.5 %copy-start.3 = (pred[512,4096]{0,1:T(8,128)(4,1)S(1)}, pred[512,4096]{0,1:T(8,128)(4,1)}, u32[]{:S(2)}) copy-start(pred[512,4096]{0,1:T(8,128)(4,1)} %iota_compare_fusion) | copy-start | bytes 6291460
  23.7 10.5 %copy-start.4 = (bf16[32,128,256]{2,1,0:T(8,128)(2,1)S(1)}, bf16[32,128,256]{2,1,0:T(8,128)(2,1)}, u32[]{:S(2)}) copy-start(bf16[32,128,256]{2,1,0:T(8,128)(2,1)} %gather_fusion) | copy-start | bytes 6291460
  23.7 20.1 %slice-start = ((s8[5242880]{0:T(1024)(128)(4,1)}), s8[4194304]{0:T(1024)(128)(4,1)S(1)}, s32[]{:S(2)}) async-start(s8[5242880]{0:T(1024)(128)(4,1)} %bitcast.104), calls=%async_computation.5 | async-start | bytes 8388608
  23.8 21.9 %slice-start.2 = ((s8[5242880]{0:T(1024)(128)(4,1)}), s8[4194304]{0:T(1024)(128)(4,1)S(1)}, s32[]{:S(2)}) async-start(s8[5242880]{0:T(1024)(128)(4,1)} %bitcast.107), calls=%async_computation.7 | async-start | bytes 8388608
  34.2 9.6 %slice-start.1 = ((s8[5242880]{0:T(1024)(128)(4,1)}), s8[1048576]{0:T(1024)(128)(4,1)S(1)}, s32[]{:S(2)}) async-start(s8[5242880]{0:T(1024)(128)(4,1)} %bitcast.104), calls=%async_computation.6 | async-start | bytes 2097152
  34.2 9.6 %slice-start.4 = ((bf16[528,512]{1,0:T(8,128)(2,1)}), bf16[16,512]{1,0:T(8,128)(2,1)S(1)}, s32[]{:S(2)}) async-start(bf16[528,512]{1,0:T(8,128)(2,1)} %param.14), calls=%async_computation.9 | async-start | bytes 32768 | tf_op jit(solution)/shard_map/slice | solution.py:34
  34.2 11.4 %slice-start.3 = ((s8[5242880]{0:T(1024)(128)(4,1)}), s8[1048576]{0:T(1024)(128)(4,1)S(1)}, s32[]{:S(2)}) async-start(s8[5242880]{0:T(1024)(128)(4,1)} %bitcast.107), calls=%async_computation.8 | async-start | bytes 2097152
  50.7 69.7 %copy-start.5 = (f32[2304]{0:T(1024)S(1)}, f32[2304]{0:T(1024)}, u32[]{:S(2)}) copy-start(f32[2304]{0:T(1024)} %param.22) | copy-start | bytes 27652
  50.8 75.5 %all-gather.6.cloned.1.call-start = ((), (), s32[]{:S(2)}) async-start(), calls=%async_computation.1 | async-start | bytes 10948608 | tf_op jit(solution)/shard_map/all_gather | solution.py:101
  51.3 123.6 %all-gather.8.cloned.1.call-start = ((), (), s32[]{:S(2)}) async-start(), calls=%async_computation.2 | async-start | bytes 10948608 | tf_op jit(solution)/shard_map/all_gather | solution.py:105
  51.9 182.7 %all-gather.10.cloned.1.call-start = ((), (), s32[]{:S(2)}) async-start(), calls=%async_computation.3 | async-start | bytes 10948608 | tf_op jit(solution)/shard_map/all_gather | solution.py:110
  52.5 287.2 %all-gather.12.cloned.1.call-start = ((), (), s32[]{:S(2)}) async-start(), calls=%async_computation.4 | async-start | bytes 12165120 | tf_op jit(solution)/shard_map/all_gather | solution.py:116
  120.5 5.8 %copy-start.7 = (f32[2304]{0:T(1024)S(1)}, f32[2304]{0:T(1024)}, u32[]{:S(2)}) copy-start(f32[2304]{0:T(1024)} %param.23) | copy-start | bytes 27652
  339.7 13.7 %copy-start.1 = (bf16[512,2304]{1,0:T(8,128)(2,1)S(1)}, bf16[512,2304]{1,0:T(8,128)(2,1)}, u32[]{:S(2)}) copy-start(bf16[512,2304]{1,0:T(8,128)(2,1)} %param.21) | copy-start | bytes 7077892
  347.3 2.4 copy-start.2
Sparse Core Ops, SparseCore 0:
  50.9 67.2 all-reduce.1
  246.4 93.2 all-gather.11
Sparse Core Ops, SparseCore 1:
  53.6 61.6 all-gather.5
  117.4 57.4 all-gather.7
  177.1 57.4 all-gather.9
